TPU v7x, 32 devices: a whole 2x2x4 slice. The times are simulated.
32 devices in a mesh: fsdp: 16 (over z, y, x), tp: 2 (over core).
Axes of the slice: x: 2, y: 2, z: 4, core: 2. Of those that a mesh axis runs over, the one named last changes fastest.
Arguments:
- hidden_in: bfloat16 [8192, 2560], P(('fsdp', 'tp')), may hold values from -67 to 67
- seq_ids: int32 [16, 512], P('fsdp'), may hold values from 0 to 1, never falling along the last dimension, each value on 1 to 384 neighbouring positions
- block_ids: int32 [16, 512], P('fsdp'), may hold values from 0 to 3, never falling along the last dimension, each value on 1 to 256 neighbouring positions
- clip_limit: float32 [1], replicated, may hold values from 6 to 12
- cotangent: bfloat16 [8192, 2560], P(('fsdp', 'tp')), may hold values from -6 to 6
- q_down: bfloat16 [2560, 768], P(('fsdp', 'tp')), may hold values from -0.125 to 0.125
- kv_down: bfloat16 [2560, 288], P(('fsdp', 'tp')), may hold values from -0.125 to 0.125
- q_up: bfloat16 [768, 3840], P('fsdp', 'tp'), may hold values from -1 to 1
- kv_up: bfloat16 [256, 5120], P('fsdp', 'tp'), may hold values from -0.375 to 0.375
- out_proj: bfloat16 [2560, 2560], P('fsdp', 'tp'), may hold values from -0.5 to 0.5
- gate_proj: bfloat16 [2560, 6400], P('fsdp', 'tp'), may hold values from -0.125 to 0.125
- up_proj: bfloat16 [2560, 6400], P('fsdp', 'tp'), may hold values from -0.125 to 0.125
- down_proj: bfloat16 [2560, 6400], P('fsdp', 'tp'), may hold values from -0.15625 to 0.15625
- in_gain: bfloat16 [2560], P(('fsdp', 'tp')), may hold values from 0.5 to 1.5
- q_gain: bfloat16 [768], P(('fsdp', 'tp')), may hold values from 0.5 to 1.5
- kv_gain: bfloat16 [256], P(('fsdp', 'tp')), may hold values from 0.5 to 1.5
- post_gain: bfloat16 [2560], P(('fsdp', 'tp')), may hold values from 0.5 to 1.5
Outputs:
- layer_out: bfloat16 [8192, 2560], P(('fsdp', 'tp'))
- input_grad: float32 [8192, 2560], P(('fsdp', 'tp'))
- q_down_grad: float32 [2560, 768], P(('fsdp', 'tp'))
- kv_down_grad: float32 [2560, 288], P(('fsdp', 'tp'))
- q_up_grad: float32 [768, 3840], P('fsdp', 'tp')
- kv_up_grad: float32 [256, 5120], P('fsdp', 'tp')
- out_proj_grad: float32 [2560, 2560], P('fsdp', 'tp')
- gate_proj_grad: float32 [2560, 6400], P('fsdp', 'tp')
- up_proj_grad: float32 [2560, 6400], P('fsdp', 'tp')
- down_proj_grad: float32 [2560, 6400], P('fsdp', 'tp')
- in_gain_grad: float32 [2560], P(('fsdp', 'tp'))
- q_gain_grad: float32 [768], P(('fsdp', 'tp'))
- kv_gain_grad: float32 [256], P(('fsdp', 'tp'))
- post_gain_grad: float32 [2560], P(('fsdp', 'tp'))
- q_up_clipped: bfloat16 [768, 3840], P('fsdp', 'tp')
- kv_up_clipped: bfloat16 [256, 5120], P('fsdp', 'tp')
- maxima: float32 [40], P('tp')
- factors: float32 [40], P('tp')
Inputs may be any that keep to these rules, and one draw needn't show every extreme that they name: `seq_ids`: along each row the ids never fall; each row holds two sequences, each of 128 to 384 tokens. `block_ids`: along each row the ids never fall; a block has 1 to 256 tokens and some block of each row has exactly 256.
All inputs are finite; a program needn't handle non-finite values.
Results may differ from a plain program's by a relative error of at most 0.014.
The roundings to bfloat16 on the way count: a program that leaves them out, or rounds other values in their place, can miss the bound.
Values may be sent and summed in bfloat16 or wider, within the bound.
A program may use at most 320 MiB of HBM per device.

v0:
```python
import functools
import math
import jax
import jax.numpy as jnp
from jax import lax
from jax.sharding import PartitionSpec as P

NOPE = 64
ROPE = 32
VD = 64
KVR = 256
eps = 1e-05
resid_scale = 1.4 / math.sqrt(62.0)
rope_base = 10000.0


def rms_scale(value, gain):
    return value * lax.rsqrt(jnp.mean(value * value, axis=-1, keepdims=True) + eps) * gain


def rotate(value, cosine, sine):
    half = value.shape[-1] // 2
    first = value[..., :half]
    second = value[..., half:]
    return jnp.concatenate(
        [first * cosine - second * sine, second * cosine + first * sine], axis=-1
    )


def angles(seq_row, start, count):
    own_ids = lax.dynamic_slice_in_dim(seq_row, start, count)
    earlier = jnp.sum((seq_row[None, :] < own_ids[:, None]).astype(jnp.int32), axis=1)
    place = (start + jnp.arange(count, dtype=jnp.int32) - earlier).astype(jnp.float32)
    freq = jnp.power(rope_base, -jnp.arange(ROPE // 2, dtype=jnp.float32) * (2.0 / ROPE))
    turn = place[:, None] * freq[None, :]
    return (jnp.cos(turn), jnp.sin(turn))


def contract(left, right, left_dim, right_dim):
    return lax.dot_general(
        left, right, (((left_dim,), (right_dim,)), ((), ())), preferred_element_type=jnp.float32
    )


def attend(items, allowed, score_scale):
    query, key_rows, value_rows = items
    raw = jnp.einsum("hqd,hkd->hqk", query, key_rows, preferred_element_type=jnp.float32)
    masked = jnp.where(allowed[None], raw * score_scale, -1e30)
    top = jnp.max(masked, axis=-1, keepdims=True)
    weights = jnp.exp(masked - top)
    total = jnp.sum(weights, axis=-1, keepdims=True)
    mixed = jnp.einsum(
        "hqk,hkd->hqd",
        (weights / total).astype(jnp.bfloat16),
        value_rows,
        preferred_element_type=jnp.float32,
    )
    return (
        mixed.astype(jnp.bfloat16),
        top[..., 0] + jnp.log(total[..., 0]),
        jnp.max(top[..., 0], axis=-1),
    )


def attend_back(items, allowed, score_scale):
    query, key_rows, value_rows, d_mixed, log_total = items
    raw = jnp.einsum("hqd,hkd->hqk", query, key_rows, preferred_element_type=jnp.float32)
    masked = jnp.where(allowed[None], raw * score_scale, -1e30)
    chance = jnp.exp(masked - log_total[..., None])
    d_values = jnp.einsum(
        "hqk,hqd->hkd", chance.astype(jnp.bfloat16), d_mixed, preferred_element_type=jnp.float32
    )
    d_chance = jnp.einsum("hqd,hkd->hqk", d_mixed, value_rows, preferred_element_type=jnp.float32)
    inner = jnp.sum(chance * d_chance, axis=-1, keepdims=True)
    d_raw = (chance * (d_chance - inner) * score_scale).astype(jnp.bfloat16)
    d_query = jnp.einsum("hqk,hkd->hqd", d_raw, key_rows, preferred_element_type=jnp.float32)
    d_key_rows = jnp.einsum("hqk,hqd->hkd", d_raw, query, preferred_element_type=jnp.float32)
    return (d_query, d_key_rows, d_values)


def shards(
    hidden_in,
    seq_ids,
    block_ids,
    clip_limit,
    cotangent,
    q_down,
    kv_down,
    q_up,
    kv_up,
    out_proj,
    gate_proj,
    up_proj,
    down_proj,
    in_gain,
    q_gain,
    kv_gain,
    post_gain,
):
    tokens_here = hidden_in.shape[0]
    seq_row = seq_ids[0]
    block_row = block_ids[0]
    group = seq_row.shape[0]
    heads = q_up.shape[1] // (NOPE + ROPE)
    stride = math.gcd(heads, 4)
    packs = heads // stride
    score_scale = 1.0 / math.sqrt(NOPE + ROPE)
    first_row = lax.axis_index("tp") * tokens_here
    q_down_full, kv_down_full, in_full, post_full, q_gain_full, kv_gain_full = (
        lax.all_gather(q_down, ("fsdp", "tp"), axis=0, tiled=True),
        lax.all_gather(kv_down, ("fsdp", "tp"), axis=0, tiled=True),
        lax.all_gather(in_gain, ("fsdp", "tp"), axis=0, tiled=True),
        lax.all_gather(post_gain, ("fsdp", "tp"), axis=0, tiled=True),
        lax.all_gather(q_gain, ("fsdp", "tp"), axis=0, tiled=True),
        lax.all_gather(kv_gain, ("fsdp", "tp"), axis=0, tiled=True),
    )
    in_float = in_full.astype(jnp.float32)
    post_float = post_full.astype(jnp.float32)
    q_gain_float = q_gain_full.astype(jnp.float32)
    kv_gain_float = kv_gain_full.astype(jnp.float32)
    q_up_full, kv_up_full, out_full, gate_full, up_full, down_full = (
        lax.all_gather(q_up, "fsdp", axis=0, tiled=True),
        lax.all_gather(kv_up, "fsdp", axis=0, tiled=True),
        lax.all_gather(out_proj, "fsdp", axis=0, tiled=True),
        lax.all_gather(gate_proj, "fsdp", axis=0, tiled=True),
        lax.all_gather(up_proj, "fsdp", axis=0, tiled=True),
        lax.all_gather(down_proj, "fsdp", axis=0, tiled=True),
    )
    x_float = hidden_in.astype(jnp.float32)
    x_normed = rms_scale(x_float, in_float).astype(jnp.bfloat16)
    q_pre = jnp.dot(x_normed, q_down_full, preferred_element_type=jnp.float32)
    c_pre = jnp.dot(x_normed, kv_down_full, preferred_element_type=jnp.float32)
    own_cos, own_sin = angles(seq_row, first_row, tokens_here)
    q_latent = rms_scale(q_pre, q_gain_float).astype(jnp.bfloat16)
    kv_latent = rms_scale(c_pre[:, :KVR], kv_gain_float).astype(jnp.bfloat16)
    key_rot = rotate(c_pre[:, KVR:], own_cos, own_sin).astype(jnp.bfloat16)
    q_lat_all, kv_lat_all, key_rot_all = (
        lax.all_gather(q_latent, "tp", axis=0, tiled=True),
        lax.all_gather(kv_latent, "tp", axis=0, tiled=True),
        lax.all_gather(key_rot, "tp", axis=0, tiled=True),
    )
    all_cos, all_sin = angles(seq_row, 0, group)
    q_full = (
        jnp.dot(q_lat_all, q_up_full, preferred_element_type=jnp.float32)
        .reshape(group, heads, NOPE + ROPE)
        .transpose(1, 0, 2)
    )
    kv_full = (
        jnp.dot(kv_lat_all, kv_up_full, preferred_element_type=jnp.float32)
        .reshape(group, heads, NOPE + VD)
        .transpose(1, 0, 2)
    )
    queries = jnp.concatenate(
        [q_full[:, :, :NOPE], rotate(q_full[:, :, NOPE:], all_cos, all_sin)], axis=-1
    ).astype(jnp.bfloat16)
    key_rows = jnp.concatenate(
        [
            kv_full[:, :, :NOPE].astype(jnp.bfloat16),
            jnp.broadcast_to(key_rot_all[None], (heads, group, ROPE)),
        ],
        axis=-1,
    )
    value_rows = kv_full[:, :, NOPE:].astype(jnp.bfloat16)
    allowed = (seq_row[:, None] == seq_row[None, :]) & (block_row[None, :] <= block_row[:, None])
    query_packs = queries.reshape(packs, stride, group, NOPE + ROPE)
    key_packs = key_rows.reshape(packs, stride, group, NOPE + ROPE)
    value_packs = value_rows.reshape(packs, stride, group, VD)
    mixed, log_total, local_peak = lax.map(
        functools.partial(attend, allowed=allowed, score_scale=score_scale),
        (query_packs, key_packs, value_packs),
    )
    attn = mixed.reshape(heads, group, VD).transpose(1, 0, 2).reshape(group, heads * VD)
    branch_part = contract(attn, out_full, 1, 1)
    branch = lax.psum_scatter(branch_part, "tp", scatter_dimension=0, tiled=True)
    mid = x_float + resid_scale * branch
    mid_normed = rms_scale(mid, post_float).astype(jnp.bfloat16)
    mid_all = lax.all_gather(mid_normed, "tp", axis=0, tiled=True)
    gate = jnp.dot(mid_all, gate_full, preferred_element_type=jnp.float32)
    up_value = jnp.dot(mid_all, up_full, preferred_element_type=jnp.float32)
    sigmoid = jax.nn.sigmoid(gate)
    silu_value = gate * sigmoid
    act = (silu_value * up_value).astype(jnp.bfloat16)
    ffn_part = contract(act, down_full, 1, 1)
    ffn = lax.psum_scatter(
        ffn_part.astype(jnp.bfloat16), "tp", scatter_dimension=0, tiled=True
    ).astype(jnp.float32)
    layer_out = (mid + resid_scale * ffn).astype(jnp.bfloat16)
    peaks = lax.pmax(local_peak.reshape(heads), "fsdp")
    limit = clip_limit[0]
    factors = limit / jnp.maximum(peaks, limit)
    root = jnp.sqrt(factors)
    q_cols = jnp.concatenate(
        [
            jnp.broadcast_to(root[:, None], (heads, NOPE)),
            jnp.broadcast_to(factors[:, None], (heads, ROPE)),
        ],
        axis=1,
    ).reshape(heads * (NOPE + ROPE))
    kv_cols = jnp.concatenate(
        [jnp.broadcast_to(root[:, None], (heads, NOPE)), jnp.ones((heads, VD), jnp.float32)], axis=1
    ).reshape(heads * (NOPE + VD))
    q_clipped = (q_up.astype(jnp.float32) * q_cols[None, :]).astype(jnp.bfloat16)
    kv_clipped = (kv_up.astype(jnp.float32) * kv_cols[None, :]).astype(jnp.bfloat16)
    q_up_back, kv_up_back, out_back, gate_back, up_back, down_back = (
        lax.all_gather(q_up, "fsdp", axis=0, tiled=True),
        lax.all_gather(kv_up, "fsdp", axis=0, tiled=True),
        lax.all_gather(out_proj, "fsdp", axis=0, tiled=True),
        lax.all_gather(gate_proj, "fsdp", axis=0, tiled=True),
        lax.all_gather(up_proj, "fsdp", axis=0, tiled=True),
        lax.all_gather(down_proj, "fsdp", axis=0, tiled=True),
    )
    cot_float = cotangent.astype(jnp.float32)
    d_ffn = (resid_scale * cot_float).astype(jnp.bfloat16)
    d_ffn_all = lax.all_gather(d_ffn, "tp", axis=0, tiled=True)
    down_grad = contract(d_ffn_all, act, 0, 0)
    d_act = jnp.dot(d_ffn_all, down_back, preferred_element_type=jnp.float32)
    d_gate = (d_act * up_value * (sigmoid * (1.0 + gate * (1.0 - sigmoid)))).astype(jnp.bfloat16)
    d_up = (d_act * silu_value).astype(jnp.bfloat16)
    gate_grad = contract(mid_all, d_gate, 0, 0)
    up_grad = contract(mid_all, d_up, 0, 0)
    d_mid_part = contract(d_gate, gate_back, 1, 1) + contract(d_up, up_back, 1, 1)
    d_mid_normed = lax.psum_scatter(d_mid_part, "tp", scatter_dimension=0, tiled=True)
    post_pull = jax.vjp(rms_scale, mid, post_float)[1]
    d_mid_norm, post_grad = post_pull(d_mid_normed)
    d_mid = cot_float + d_mid_norm
    d_branch = (resid_scale * d_mid).astype(jnp.bfloat16)
    d_branch_all = lax.all_gather(d_branch, "tp", axis=0, tiled=True)
    out_grad = contract(d_branch_all, attn, 0, 0)
    d_attn = jnp.dot(d_branch_all, out_back, preferred_element_type=jnp.float32).astype(
        jnp.bfloat16
    )
    d_mixed = d_attn.reshape(group, heads, VD).transpose(1, 0, 2).reshape(packs, stride, group, VD)
    d_query, d_key_rows, d_values = lax.map(
        functools.partial(attend_back, allowed=allowed, score_scale=score_scale),
        (query_packs, key_packs, value_packs, d_mixed, log_total),
    )
    d_query = d_query.reshape(heads, group, NOPE + ROPE)
    d_key_rows = d_key_rows.reshape(heads, group, NOPE + ROPE)
    d_values = d_values.reshape(heads, group, VD)
    d_q_rot = rotate(d_query[:, :, NOPE:], all_cos, -all_sin)
    d_q = (
        jnp.concatenate([d_query[:, :, :NOPE], d_q_rot], axis=-1)
        .transpose(1, 0, 2)
        .reshape(group, heads * (NOPE + ROPE))
        .astype(jnp.bfloat16)
    )
    d_key_rot_part = jnp.sum(d_key_rows[:, :, NOPE:], axis=0)
    d_kv = (
        jnp.concatenate([d_key_rows[:, :, :NOPE], d_values], axis=-1)
        .transpose(1, 0, 2)
        .reshape(group, heads * (NOPE + VD))
        .astype(jnp.bfloat16)
    )
    q_up_grad = contract(q_lat_all, d_q, 0, 0)
    kv_up_grad = contract(kv_lat_all, d_kv, 0, 0)
    d_q_lat_part = contract(d_q, q_up_back, 1, 1)
    d_kv_lat_part = contract(d_kv, kv_up_back, 1, 1)
    d_q_latent, d_kv_latent, d_key_rot = (
        lax.psum_scatter(d_q_lat_part, "tp", scatter_dimension=0, tiled=True),
        lax.psum_scatter(d_kv_lat_part, "tp", scatter_dimension=0, tiled=True),
        lax.psum_scatter(d_key_rot_part, "tp", scatter_dimension=0, tiled=True),
    )
    q_pull = jax.vjp(rms_scale, q_pre, q_gain_float)[1]
    d_q_pre_float, q_gain_grad = q_pull(d_q_latent)
    kv_pull = jax.vjp(rms_scale, c_pre[:, :KVR], kv_gain_float)[1]
    d_c_lat, kv_gain_grad = kv_pull(d_kv_latent)
    d_c_pre = jnp.concatenate([d_c_lat, rotate(d_key_rot, own_cos, -own_sin)], axis=-1).astype(
        jnp.bfloat16
    )
    d_q_pre = d_q_pre_float.astype(jnp.bfloat16)
    q_down_grad = contract(x_normed, d_q_pre, 0, 0)
    kv_down_grad = contract(x_normed, d_c_pre, 0, 0)
    d_x_normed = contract(d_q_pre, q_down_full, 1, 1) + contract(d_c_pre, kv_down_full, 1, 1)
    in_pull = jax.vjp(rms_scale, x_float, in_float)[1]
    d_x_norm, in_grad = in_pull(d_x_normed)
    input_grad = d_mid + d_x_norm
    q_down_out, kv_down_out, in_out, post_out, q_gain_out, kv_gain_out = (
        lax.psum_scatter(q_down_grad, ("fsdp", "tp"), scatter_dimension=0, tiled=True),
        lax.psum_scatter(kv_down_grad, ("fsdp", "tp"), scatter_dimension=0, tiled=True),
        lax.psum_scatter(in_grad, ("fsdp", "tp"), scatter_dimension=0, tiled=True),
        lax.psum_scatter(post_grad, ("fsdp", "tp"), scatter_dimension=0, tiled=True),
        lax.psum_scatter(q_gain_grad, ("fsdp", "tp"), scatter_dimension=0, tiled=True),
        lax.psum_scatter(kv_gain_grad, ("fsdp", "tp"), scatter_dimension=0, tiled=True),
    )
    q_up_out, kv_up_out, out_out, gate_out, up_out, down_out = (
        lax.psum_scatter(q_up_grad, "fsdp", scatter_dimension=0, tiled=True),
        lax.psum_scatter(kv_up_grad, "fsdp", scatter_dimension=0, tiled=True),
        lax.psum_scatter(out_grad, "fsdp", scatter_dimension=0, tiled=True),
        lax.psum_scatter(gate_grad, "fsdp", scatter_dimension=0, tiled=True),
        lax.psum_scatter(up_grad, "fsdp", scatter_dimension=0, tiled=True),
        lax.psum_scatter(down_grad, "fsdp", scatter_dimension=0, tiled=True),
    )
    return (
        layer_out,
        input_grad,
        q_down_out,
        kv_down_out,
        q_up_out,
        kv_up_out,
        out_out,
        gate_out,
        up_out,
        down_out,
        in_out,
        q_gain_out,
        kv_gain_out,
        post_out,
        q_clipped,
        kv_clipped,
        peaks,
        factors,
    )


def solution(mesh):
    placed = (
        P(("fsdp", "tp"), None),
        P("fsdp", None),
        P("fsdp", None),
        P(),
        P(("fsdp", "tp"), None),
        P(("fsdp", "tp"), None),
        P(("fsdp", "tp"), None),
        P("fsdp", "tp"),
        P("fsdp", "tp"),
        P("fsdp", "tp"),
        P("fsdp", "tp"),
        P("fsdp", "tp"),
        P("fsdp", "tp"),
        P(("fsdp", "tp")),
        P(("fsdp", "tp")),
        P(("fsdp", "tp")),
        P(("fsdp", "tp")),
    )
    return jax.shard_map(
        shards,
        mesh=mesh,
        in_specs=placed,
        out_specs=(
            P(("fsdp", "tp"), None),
            P(("fsdp", "tp"), None),
            P(("fsdp", "tp"), None),
            P(("fsdp", "tp"), None),
            P("fsdp", "tp"),
            P("fsdp", "tp"),
            P("fsdp", "tp"),
            P("fsdp", "tp"),
            P("fsdp", "tp"),
            P("fsdp", "tp"),
            P(("fsdp", "tp")),
            P(("fsdp", "tp")),
            P(("fsdp", "tp")),
            P(("fsdp", "tp")),
            P("fsdp", "tp"),
            P("fsdp", "tp"),
            P("tp"),
            P("tp"),
        ),
        check_vma=False,
    )
```

profile of v0, /device:TPU:10, one launch (start us, length us, event | category | flops | bytes accessed | tf_op | source)
XLA Modules:
  0.0 4047.5 jit_solution(4682745554615388410)
XLA Ops:
  14.1 41.7 %all-reduce.10 = (bf16[2560]{0:T(1024)(128)(2,1)S(1)}, bf16[768]{0:T(1024)(128)(2,1)S(1)}, bf16[256]{0:T(256)(128)(2,1)S(1)}, bf16[2560]{0:T(1024)(128)(2,1)S(1)}) all-reduce(bf16[2560]{0:T(1024)(128)(2,1)S(1)} %dynamic-update-slice, bf16[768]{0:T(1024)(128)(2,1)S(1)} %dynamic-update-slice.1, ...), channel_id=1, replica_groups=mesh['fsdp'=16,'tp'=2] {'fsdp','tp'}, use_global_device_ids=true, to_apply=%add.1 | all-reduce | flops 6144 | bytes 24576
  72.9 52.5 %all-gather.18.cloned.1.call-done = bf16[256,2560]{1,0:T(8,128)(2,1)} async-done(((bf16[16,2560]{1,0:T(8,128)(2,1)}), bf16[256,2560]{1,0:T(8,128)(2,1)}) %all-gather.18.cloned.1.call-update) | async-done | bytes 1310736 | tf_op jit(solution)/shard_map/all_gather | solution.py:123
  135.3 54.2 %all-gather.12.cloned.1.call-done = bf16[2560,768]{1,0:T(8,128)(2,1)} async-done(((bf16[80,768]{1,0:T(8,128)(2,1)}), bf16[2560,768]{1,0:T(8,128)(2,1)}) %all-gather.12.cloned.1.call-update) | async-done | bytes 3932176 | tf_op jit(solution)/shard_map/all_gather | solution.py:110
  196.9 60.9 %all-gather.14.cloned.1.call-done = bf16[768,1920]{1,0:T(8,128)(2,1)} async-done(((bf16[48,1920]{1,0:T(8,128)(2,1)}), bf16[768,1920]{1,0:T(8,128)(2,1)}) %all-gather.14.cloned.1.call-update) | async-done | bytes 2949136 | tf_op jit(solution)/shard_map/all_gather | solution.py:122
  263.6 40.1 while.30
  303.7 51.2 %all-gather.20.cloned.1.call-done = bf16[2560,1280]{1,0:T(8,128)(2,1)} async-done(((bf16[160,1280]{1,0:T(8,128)(2,1)}), bf16[2560,1280]{1,0:T(8,128)(2,1)}) %all-gather.20.cloned.1.call-update) | async-done | bytes 6553616 | tf_op jit(solution)/shard_map/all_gather | solution.py:124
  394.6 190.1 %all-gather.24.cloned.1.call-done = bf16[2560,3200]{1,0:T(8,128)(2,1)} async-done(((bf16[160,3200]{1,0:T(8,128)(2,1)}), bf16[2560,3200]{1,0:T(8,128)(2,1)}) %all-gather.24.cloned.1.call-update) | async-done | bytes 16384016 | tf_op jit(solution)/shard_map/all_gather | solution.py:125
  600.4 173.6 %all-gather.26.cloned.1.call-done = bf16[2560,3200]{1,0:T(8,128)(2,1)} async-done(((bf16[160,3200]{1,0:T(8,128)(2,1)}), bf16[2560,3200]{1,0:T(8,128)(2,1)}) %all-gather.26.cloned.1.call-update) | async-done | bytes 16384016 | tf_op jit(solution)/shard_map/all_gather | solution.py:126
  788.9 188.3 %all-gather.28.cloned.1.call-done = bf16[2560,3200]{1,0:T(8,128)(2,1)} async-done(((bf16[160,3200]{1,0:T(8,128)(2,1)}), bf16[2560,3200]{1,0:T(8,128)(2,1)}) %all-gather.28.cloned.1.call-update) | async-done | bytes 16384016 | tf_op jit(solution)/shard_map/all_gather | solution.py:127
  977.2 21.1 multiply_convert_fusion.1
  998.3 16.1 fusion.127
  1071.4 137.5 %while.31 = (s32[]{:T(128)}, f32[5,4,512,96]{2,3,1,0:T(8,128)}, f32[5,4,512,96]{2,3,1,0:T(8,128)}, bf16[5,4,512,64]{2,3,1,0:T(8,128)(2,1)S(1)}, bf16[5,4,512,96]...) while((s32[]{:T(128)}, f32[5,4,512,96]{2,3,1,0:T(8,128)}, ...), condition=%wide.region_17.18_spmd.clone, body=%wide.region_15.17_spmd.clone.sunk | while | flops 887886848 | bytes 51151992 | solution.py:233
  1276.7 18.2 fusion.133
  1294.9 17.7 fusion.134
  1313.0 17.9 fusion.135
  1331.7 31.0 pmax.7
  1370.9 51.4 %all-reduce.9 = (f32[2560]{0:T(1024)S(1)}, f32[768]{0:T(1024)S(1)}, f32[256]{0:T(256)S(1)}, f32[2560]{0:T(1024)S(1)}) all-reduce(f32[2560]{0:T(1024)S(1)} %get-tuple-element.174, f32[768]{0:T(1024)S(1)} %get-tuple-element.176, f32[256]{0:T(256)S(1)} %get-tuple-element.178, ...), channel_id=16, replica_groups=mesh['fsdp'=16,'tp'=2] {'fsdp','tp'}, use_global_device_ids=true, to_apply=%region_34.35.clone | all-reduce | flops 6144 | bytes 49152
  1430.6 17.7 reduce-scatter.33.cloned.1.call-done
  1448.2 155.2 %reduce-scatter.31.cloned.1.call-done = f32[48,1920]{1,0:T(8,128)} async-done(((f32[768,1920]{1,0:T(8,128)}), f32[48,1920]{1,0:T(8,128)}) %reduce-scatter.31.cloned.1.call-update) | async-done | bytes 368656 | tf_op jit(solution)/shard_map/reduce_scatter | solution.py:286
  1603.5 129.2 %reduce-scatter.27.cloned.1.call-done = f32[80,768]{1,0:T(8,128)} async-done(((f32[2560,768]{1,0:T(8,128)}), f32[80,768]{1,0:T(8,128)}) %reduce-scatter.27.cloned.1.call-update) | async-done | bytes 245776 | tf_op jit(solution)/shard_map/reduce_scatter | solution.py:278
  1732.6 279.7 %reduce-scatter.35.cloned.1.call-done = f32[160,1280]{1,0:T(8,128)} async-done(((f32[2560,1280]{1,0:T(8,128)}), f32[160,1280]{1,0:T(8,128)}) %reduce-scatter.35.cloned.1.call-update) | async-done | bytes 819216 | tf_op jit(solution)/shard_map/reduce_scatter | solution.py:288
  2012.3 676.1 %reduce-scatter.37.cloned.1.call-done = f32[160,3200]{1,0:T(8,128)} async-done(((f32[2560,3200]{1,0:T(8,128)}), f32[160,3200]{1,0:T(8,128)}) %reduce-scatter.37.cloned.1.call-update) | async-done | bytes 2048016 | tf_op jit(solution)/shard_map/reduce_scatter | solution.py:289
  2688.5 676.1 %reduce-scatter.39.cloned.1.call-done = f32[160,3200]{1,0:T(8,128)} async-done(((f32[2560,3200]{1,0:T(8,128)}), f32[160,3200]{1,0:T(8,128)}) %reduce-scatter.39.cloned.1.call-update) | async-done | bytes 2048016 | tf_op jit(solution)/shard_map/reduce_scatter | solution.py:290
  3364.6 676.1 %reduce-scatter.41.cloned.1.call-done = f32[160,3200]{1,0:T(8,128)} async-done(((f32[2560,3200]{1,0:T(8,128)}), f32[160,3200]{1,0:T(8,128)}) %reduce-scatter.41.cloned.1.call-update) | async-done | bytes 2048016 | tf_op jit(solution)/shard_map/reduce_scatter | solution.py:291
  (351 shorter events, 435.3 us)
Async XLA Ops:
  7.2 60.1 %all-gather.16.cloned.1.call-start = ((), (), s32[]{:S(2)}) async-start(), calls=%async_computation.16 | async-start | bytes 2027520 | tf_op jit(solution)/shard_map/all_gather | solution.py:111
  7.9 117.5 %all-gather.18.cloned.1.call-start = ((), (), s32[]{:S(2)}) async-start(), calls=%async_computation.17 | async-start | bytes 1392640 | tf_op jit(solution)/shard_map/all_gather | solution.py:123
  8.7 180.8 %all-gather.12.cloned.1.call-start = ((), (), s32[]{:S(2)}) async-start(), calls=%async_computation.14 | async-start | bytes 4055040 | tf_op jit(solution)/shard_map/all_gather | solution.py:110
  9.4 248.5 %all-gather.14.cloned.1.call-start = ((), (), s32[]{:S(2)}) async-start(), calls=%async_computation.15 | async-start | bytes 3133440 | tf_op jit(solution)/shard_map/all_gather | solution.py:122
  10.0 344.9 %all-gather.20.cloned.1.call-start = ((), (), s32[]{:S(2)}) async-start(), calls=%async_computation.18 | async-start | bytes 6963200 | tf_op jit(solution)/shard_map/all_gather | solution.py:124
  10.6 366.2 %reduce-scatter.15.cloned.1.call-start = ((), (), s32[]{:S(2)}) async-start(), calls=%async_computation.19 | async-start | bytes 7864320 | tf_op jit(solution)/shard_map/reduce_scatter | solution.py:174
  364.1 30.5 all-gather.22.cloned.1.call-start
  382.0 202.7 %all-gather.24.cloned.1.call-start = ((), (), s32[]{:S(2)}) async-start(), calls=%async_computation.21 | async-start | bytes 17408000 | tf_op jit(solution)/shard_map/all_gather | solution.py:125
  382.7 391.2 %all-gather.26.cloned.1.call-start = ((), (), s32[]{:S(2)}) async-start(), calls=%async_computation.22 | async-start | bytes 17408000 | tf_op jit(solution)/shard_map/all_gather | solution.py:126
  383.5 405.5 %all-gather.30.cloned.1.call-start = ((), (), s32[]{:S(2)}) async-start(), calls=%async_computation.25 | async-start | bytes 3932160 | tf_op jit(solution)/shard_map/all_gather | solution.py:214
  384.8 592.4 %all-gather.28.cloned.1.call-start = ((), (), s32[]{:S(2)}) async-start(), calls=%async_computation.23 | async-start | bytes 17408000 | tf_op jit(solution)/shard_map/all_gather | solution.py:127
  385.6 657.4 %reduce-scatter.19.cloned.1.call-start = ((), (), s32[]{:S(2)}) async-start(), calls=%async_computation.26 | async-start | bytes 7864320 | tf_op jit(solution)/shard_map/reduce_scatter | solution.py:222
  1029.3 31.8 all-gather.32.cloned.1.call-start
  1048.4 190.1 %reduce-scatter.25.cloned.1.call-start = ((), (), s32[]{:S(2)}) async-start(), calls=%async_computation.30 | async-start | bytes 98304 | tf_op jit(solution)/shard_map/reduce_scatter | solution.py:261
  1216.4 41.2 %reduce-scatter.21.cloned.1.call-start = ((), (), s32[]{:S(2)}) async-start(), calls=%async_computation.28 | async-start | bytes 2359296 | tf_op jit(solution)/shard_map/reduce_scatter | solution.py:259
  1224.5 200.2 %reduce-scatter.17.cloned.1.call-start = ((), (), s32[]{:S(2)}) async-start(), calls=%async_computation.24 | async-start | bytes 3932160 | tf_op jit(solution)/shard_map/reduce_scatter | solution.py:184
  1238.3 192.3 %reduce-scatter.29.cloned.1.call-start = ((), (), s32[]{:S(2)}) async-start(), calls=%async_computation.32 | async-start | bytes 4055040 | tf_op jit(solution)/shard_map/reduce_scatter | solution.py:279
  1244.9 203.4 %reduce-scatter.33.cloned.1.call-start = ((), (), s32[]{:S(2)}) async-start(), calls=%async_computation.34 | async-start | bytes 2785280 | tf_op jit(solution)/shard_map/reduce_scatter | solution.py:287
  1250.1 353.4 %reduce-scatter.31.cloned.1.call-start = ((), (), s32[]{:S(2)}) async-start(), calls=%async_computation.33 | async-start | bytes 6266880 | tf_op jit(solution)/shard_map/reduce_scatter | solution.py:286
  1257.5 475.1 %reduce-scatter.27.cloned.1.call-start = ((), (), s32[]{:S(2)}) async-start(), calls=%async_computation.31 | async-start | bytes 8110080 | tf_op jit(solution)/shard_map/reduce_scatter | solution.py:278
  1265.9 746.4 %reduce-scatter.35.cloned.1.call-start = ((), (), s32[]{:S(2)}) async-start(), calls=%async_computation.35 | async-start | bytes 13926400 | tf_op jit(solution)/shard_map/reduce_scatter | solution.py:288
  1276.4 1412.0 %reduce-scatter.37.cloned.1.call-start = ((), (), s32[]{:S(2)}) async-start(), calls=%async_computation.36 | async-start | bytes 34816000 | tf_op jit(solution)/shard_map/reduce_scatter | solution.py:289
  1294.9 2069.7 %reduce-scatter.39.cloned.1.call-start = ((), (), s32[]{:S(2)}) async-start(), calls=%async_computation.37 | async-start | bytes 34816000 | tf_op jit(solution)/shard_map/reduce_scatter | solution.py:290
  1312.7 2728.0 %reduce-scatter.41.cloned.1.call-start = ((), (), s32[]{:S(2)}) async-start(), calls=%async_computation.38 | async-start | bytes 34816000 | tf_op jit(solution)/shard_map/reduce_scatter | solution.py:291
  (64 other events, 3252.0 us)
Sparse Core Ops, SparseCore 0:
  10.9 56.2 all-gather.15
  70.0 55.3 all-gather.17
  128.3 61.0 all-gather.11
  192.1 65.7 all-gather.13
  260.4 94.4 all-gather.19
  364.2 12.5 reduce-scatter.14
  382.1 12.4 all-gather.21
  397.7 186.9 all-gather.23
  587.8 186.1 all-gather.25
  775.4 11.6 all-gather.29
  790.2 186.9 all-gather.27
  1029.4 13.5 reduce-scatter.18
  1048.5 12.5 all-gather.31
  1224.3 9.1 reduce-scatter.22
  1236.2 10.2 reduce-scatter.20
  1248.6 11.4 reduce-scatter.16
  1266.8 104.8 reduce-scatter.28
  1374.7 73.4 reduce-scatter.32
  1454.8 148.5 reduce-scatter.30
  1610.7 121.9 reduce-scatter.26
  1735.5 276.7 reduce-scatter.34
  2015.3 673.1 reduce-scatter.36
  2691.4 673.1 reduce-scatter.38
  3367.5 673.1 reduce-scatter.40
  (1 shorter events, 8.5 us)
where the time goes:
time: 4050 us
  waiting for transfers between devices  3440 us (85%)
  matrix products  380 us (9%)
  blocking collectives  131 us (3%)
  other arithmetic  44.1 us (1%)
    reduce_scatter x1, waiting for transfers between devices, shards(): lax.psum_scatter(gate_grad, 'fsdp', scatter_dimension=0, tiled=True)  676 us
    reduce_scatter x1, waiting for transfers between devices, shards(): lax.psum_scatter(down_grad, 'fsdp', scatter_dimension=0, tiled=True)  676 us
    reduce_scatter x1, waiting for transfers between devices, shards(): lax.psum_scatter(up_grad, 'fsdp', scatter_dimension=0, tiled=True)  676 us
    reduce_scatter x1, waiting for transfers between devices, shards(): lax.psum_scatter(out_grad, 'fsdp', scatter_dimension=0, tiled=True)  280 us
    all_gather x1, waiting for transfers between devices, shards(): lax.all_gather(gate_proj, 'fsdp', axis=0, tiled=True)  190 us
    all_gather x1, waiting for transfers between devices, shards(): lax.all_gather(down_proj, 'fsdp', axis=0, tiled=True)  188 us
    all_gather x1, waiting for transfers between devices, shards(): lax.all_gather(up_proj, 'fsdp', axis=0, tiled=True)  174 us
    reduce_scatter x1, waiting for transfers between devices, shards(): lax.psum_scatter(q_up_grad, 'fsdp', scatter_dimension=0, tiled=True)  155 us
  transfers between devices with their start and end apart: 25, of which 19 were waited for; matrix products, arithmetic and copies ran while one was open for 6% of the time, Pallas kernels for 0%

commit v1 on v0

--- a/solution.py
+++ b/solution.py
@@ -12,6 +12,27 @@
 eps = 1e-05
 resid_scale = 1.4 / math.sqrt(62.0)
 rope_base = 10000.0
+
+
+def collect(x, axis, dim):
+    devices, place, rows = (lax.axis_size(axis), lax.axis_index(axis), x.shape[dim])
+    right = [(i, (i + 1) % devices) for i in range(devices)]
+    downward = [(i, (i - 1) % devices) for i in range(devices)]
+    filled = jnp.zeros((*x.shape[:dim], devices * rows, *x.shape[dim + 1 :]), x.dtype)
+    filled = lax.dynamic_update_slice_in_dim(filled, x, place * rows, axis=dim)
+    from_left = from_right = x
+    middle = devices // 2
+    for step in range(1, middle + 1):
+        from_left = lax.ppermute(from_left, axis, right)
+        filled = lax.dynamic_update_slice_in_dim(
+            filled, from_left, (place - step) % devices * rows, axis=dim
+        )
+        if step < devices - middle:
+            from_right = lax.ppermute(from_right, axis, downward)
+            filled = lax.dynamic_update_slice_in_dim(
+                filled, from_right, (place + step) % devices * rows, axis=dim
+            )
+    return filled
 
 
 def rms_scale(value, gain):
@@ -123,7 +144,7 @@
         lax.all_gather(kv_up, "fsdp", axis=0, tiled=True),
         lax.all_gather(out_proj, "fsdp", axis=0, tiled=True),
         lax.all_gather(gate_proj, "fsdp", axis=0, tiled=True),
-        lax.all_gather(up_proj, "fsdp", axis=0, tiled=True),
+        collect(up_proj, "fsdp", 0),
         lax.all_gather(down_proj, "fsdp", axis=0, tiled=True),
     )
     x_float = hidden_in.astype(jnp.float32)

time: 4050 us -> 4220 us (1.042)
  waiting for transfers between devices: 3440 us -> 3560 us
    ppermute x0 -> x15, waiting for transfers between devices: none -> 396 us  [the longest x8 358 us: collect(): from_left = lax.ppermute(from_left, axis, right)]
    all_gather x1, waiting for transfers between devices: 190 us -> 0.01 us  [shards(): lax.all_gather(gate_proj, 'fsdp', axis=0, tiled=True)]
  transfers between devices with their start and end apart: 25 -> 40, of which waited for: 19 -> 30; matrix products, arithmetic and copies ran while one was open for 6% -> 7% of each run, Pallas kernels for 0% -> 0%
where the time goes in v1:
time: 4220 us
  waiting for transfers between devices  3560 us (84%)
  matrix products  380 us (9%)
  blocking collectives  131 us (3%)
  local copies, waits for them, and re-layouts  66 us (2%)
  other arithmetic  47.1 us (1%)
    reduce_scatter x1, waiting for transfers between devices, shards(): lax.psum_scatter(down_grad, 'fsdp', scatter_dimension=0, tiled=True)  676 us
    reduce_scatter x1, waiting for transfers between devices, shards(): lax.psum_scatter(up_grad, 'fsdp', scatter_dimension=0, tiled=True)  676 us
    reduce_scatter x1, waiting for transfers between devices, shards(): lax.psum_scatter(gate_grad, 'fsdp', scatter_dimension=0, tiled=True)  676 us
    ppermute x8, waiting for transfers between devices, collect(): from_left = lax.ppermute(from_left, axis, right)  358 us
    reduce_scatter x1, waiting for transfers between devices, shards(): lax.psum_scatter(out_grad, 'fsdp', scatter_dimension=0, tiled=True)  280 us
    reduce_scatter x1, waiting for transfers between devices, shards(): lax.psum_scatter(q_up_grad, 'fsdp', scatter_dimension=0, tiled=True)  156 us
    all_gather x1, waiting for transfers between devices, shards(): lax.all_gather(down_proj, 'fsdp', axis=0, tiled=True)  151 us
    dot_general x16, matrix products, contract(): lax.dot_general(left, right, (((left_dim,), (right_dim,)), ((), ())), pre...  146 us
  transfers between devices with their start and end apart: 40, of which 30 were waited for; matrix products, arithmetic and copies ran while one was open for 7% of the time, Pallas kernels for 0%

profile of v1, /device:TPU:10, one launch (start us, length us, event | category | flops | bytes accessed | tf_op | source)
XLA Modules:
  0.0 4217.2 jit_solution(1948138934088579117)
XLA Ops:
  16.7 41.8 all-reduce.10
  73.1 52.5 %all-gather.18.cloned.1.call-done = bf16[256,2560]{1,0:T(8,128)(2,1)} async-done(((bf16[16,2560]{1,0:T(8,128)(2,1)}), bf16[256,2560]{1,0:T(8,128)(2,1)}) %all-gather.18.cloned.1.call-update) | async-done | bytes 1310736 | tf_op jit(solution)/shard_map/all_gather | solution.py:144
  135.4 54.2 %all-gather.12.cloned.1.call-done = bf16[2560,768]{1,0:T(8,128)(2,1)} async-done(((bf16[80,768]{1,0:T(8,128)(2,1)}), bf16[2560,768]{1,0:T(8,128)(2,1)}) %all-gather.12.cloned.1.call-update) | async-done | bytes 3932176 | tf_op jit(solution)/shard_map/all_gather | solution.py:131
  196.7 61.3 %all-gather.14.cloned.1.call-done = bf16[768,1920]{1,0:T(8,128)(2,1)} async-done(((bf16[48,1920]{1,0:T(8,128)(2,1)}), bf16[768,1920]{1,0:T(8,128)(2,1)}) %all-gather.14.cloned.1.call-update) | async-done | bytes 2949136 | tf_op jit(solution)/shard_map/all_gather | solution.py:143
  263.8 43.1 %while.30 = (s32[]{:T(128)}, bf16[5,4,512,64]{2,3,1,0:T(8,128)(2,1)}, f32[5,4,512]{2,1,0:T(4,128)}, f32[5,4]{1,0:T(8,128)}, bf16[5,4,512,96]{2,3,1,0:T(8,128)(2,...) while((s32[]{:T(128)}, ...), condition=%wide.region_9.10_spmd.clone, body=%wide.region_5.9_spmd.clone.sunk | while | flops 350091264 | bytes 15014561 | solution.py:189
  306.8 48.3 %all-gather.20.cloned.1.call-done = bf16[2560,1280]{1,0:T(8,128)(2,1)} async-done(((bf16[160,1280]{1,0:T(8,128)(2,1)}), bf16[2560,1280]{1,0:T(8,128)(2,1)}) %all-gather.20.cloned.1.call-update) | async-done | bytes 6553616 | tf_op jit(solution)/shard_map/all_gather | solution.py:145
  387.8 52.0 %collective-permute-done = bf16[160,3200]{1,0:T(8,128)(2,1)S(1)} collective-permute-done((bf16[160,3200]{1,0:T(8,128)(2,1)S(1)}, bf16[160,3200]{1,0:T(8,128)(2,1)S(1)}, u32[]{:S(2)}, u32[]{:S(2)}) %collective-permute-start) | collective-permute-done | bytes 1024032 | tf_op jit(solution)/shard_map/ppermute | solution.py:26
  441.9 66.1 %collective-permute-done.2 = bf16[160,3200]{1,0:T(8,128)(2,1)} collective-permute-done((bf16[160,3200]{1,0:T(8,128)(2,1)S(1)}, bf16[160,3200]{1,0:T(8,128)(2,1)}, u32[]{:S(2)}, u32[]{:S(2)}) %collective-permute-start.2) | collective-permute-done | bytes 1024032 | tf_op jit(solution)/shard_map/ppermute | solution.py:26
  516.6 42.3 %collective-permute-done.4 = bf16[160,3200]{1,0:T(8,128)(2,1)S(1)} collective-permute-done((bf16[160,3200]{1,0:T(8,128)(2,1)}, bf16[160,3200]{1,0:T(8,128)(2,1)S(1)}, u32[]{:S(2)}, u32[]{:S(2)}) %collective-permute-start.4) | collective-permute-done | bytes 1024032 | tf_op jit(solution)/shard_map/ppermute | solution.py:26
  572.7 48.0 %collective-permute-done.6 = bf16[160,3200]{1,0:T(8,128)(2,1)} collective-permute-done((bf16[160,3200]{1,0:T(8,128)(2,1)S(1)}, bf16[160,3200]{1,0:T(8,128)(2,1)}, u32[]{:S(2)}, u32[]{:S(2)}) %collective-permute-start.6) | collective-permute-done | bytes 1024032 | tf_op jit(solution)/shard_map/ppermute | solution.py:26
  647.1 45.5 %collective-permute-done.8 = bf16[160,3200]{1,0:T(8,128)(2,1)S(1)} collective-permute-done((bf16[160,3200]{1,0:T(8,128)(2,1)}, bf16[160,3200]{1,0:T(8,128)(2,1)S(1)}, u32[]{:S(2)}, u32[]{:S(2)}) %collective-permute-start.8) | collective-permute-done | bytes 1024032 | tf_op jit(solution)/shard_map/ppermute | solution.py:26
  710.1 40.5 collective-permute-done.10
  755.7 38.7 collective-permute-done.12
  840.2 151.1 %all-gather.26.cloned.1.call-done = bf16[2560,3200]{1,0:T(8,128)(2,1)} async-done(((bf16[160,3200]{1,0:T(8,128)(2,1)}), bf16[2560,3200]{1,0:T(8,128)(2,1)}) %all-gather.26.cloned.1.call-update) | async-done | bytes 16384016 | tf_op jit(solution)/shard_map/all_gather | solution.py:148
  1042.7 137.7 %all-gather.30.cloned.1.call-done = bf16[2560,3200]{1,0:T(8,128)(2,1)} async-done(((bf16[160,3200]{1,0:T(8,128)(2,1)}), bf16[2560,3200]{1,0:T(8,128)(2,1)}) %all-gather.30.cloned.1.call-update) | async-done | bytes 16384016 | tf_op jit(solution)/shard_map/all_gather | solution.py:230
  1237.2 141.3 %while.31 = (s32[]{:T(128)}, f32[5,4,512,96]{2,3,1,0:T(8,128)}, f32[5,4,512,96]{2,3,1,0:T(8,128)}, bf16[5,4,512,64]{2,3,1,0:T(8,128)(2,1)S(1)}, bf16[5,4,512,96]...) while((s32[]{:T(128)}, f32[5,4,512,96]{2,3,1,0:T(8,128)}, ...), condition=%wide.region_17.18_spmd.clone, body=%wide.region_15.17_spmd.clone.sunk | while | flops 887886848 | bytes 51151992 | solution.py:254
  1501.6 31.1 pmax.7
  1540.9 51.7 %all-reduce.9 = (f32[2560]{0:T(1024)S(1)}, f32[768]{0:T(1024)S(1)}, f32[256]{0:T(256)S(1)}, f32[2560]{0:T(1024)S(1)}) all-reduce(f32[2560]{0:T(1024)S(1)} %get-tuple-element.174, f32[768]{0:T(1024)S(1)} %get-tuple-element.176, f32[256]{0:T(256)S(1)} %get-tuple-element.178, ...), channel_id=16, replica_groups=mesh['fsdp'=16,'tp'=2] {'fsdp','tp'}, use_global_device_ids=true, to_apply=%region_34.35.clone | all-reduce | flops 6144 | bytes 49152
  1617.5 155.9 %reduce-scatter.31.cloned.1.call-done = f32[48,1920]{1,0:T(8,128)} async-done(((f32[768,1920]{1,0:T(8,128)}), f32[48,1920]{1,0:T(8,128)}) %reduce-scatter.31.cloned.1.call-update) | async-done | bytes 368656 | tf_op jit(solution)/shard_map/reduce_scatter | solution.py:307
  1773.4 129.0 %reduce-scatter.27.cloned.1.call-done = f32[80,768]{1,0:T(8,128)} async-done(((f32[2560,768]{1,0:T(8,128)}), f32[80,768]{1,0:T(8,128)}) %reduce-scatter.27.cloned.1.call-update) | async-done | bytes 245776 | tf_op jit(solution)/shard_map/reduce_scatter | solution.py:299
  1902.4 279.7 %reduce-scatter.35.cloned.1.call-done = f32[160,1280]{1,0:T(8,128)} async-done(((f32[2560,1280]{1,0:T(8,128)}), f32[160,1280]{1,0:T(8,128)}) %reduce-scatter.35.cloned.1.call-update) | async-done | bytes 819216 | tf_op jit(solution)/shard_map/reduce_scatter | solution.py:309
  2182.1 676.1 %reduce-scatter.37.cloned.1.call-done = f32[160,3200]{1,0:T(8,128)} async-done(((f32[2560,3200]{1,0:T(8,128)}), f32[160,3200]{1,0:T(8,128)}) %reduce-scatter.37.cloned.1.call-update) | async-done | bytes 2048016 | tf_op jit(solution)/shard_map/reduce_scatter | solution.py:310
  2858.2 676.1 %reduce-scatter.39.cloned.1.call-done = f32[160,3200]{1,0:T(8,128)} async-done(((f32[2560,3200]{1,0:T(8,128)}), f32[160,3200]{1,0:T(8,128)}) %reduce-scatter.39.cloned.1.call-update) | async-done | bytes 2048016 | tf_op jit(solution)/shard_map/reduce_scatter | solution.py:311
  3534.4 676.2 %reduce-scatter.41.cloned.1.call-done = f32[160,3200]{1,0:T(8,128)} async-done(((f32[2560,3200]{1,0:T(8,128)}), f32[160,3200]{1,0:T(8,128)}) %reduce-scatter.41.cloned.1.call-update) | async-done | bytes 2048016 | tf_op jit(solution)/shard_map/reduce_scatter | solution.py:312
  (410 shorter events, 645.2 us)
Async XLA Ops:
  7.9 117.7 %all-gather.18.cloned.1.call-start = ((), (), s32[]{:S(2)}) async-start(), calls=%async_computation.17 | async-start | bytes 1392640 | tf_op jit(solution)/shard_map/all_gather | solution.py:144
  8.7 180.9 %all-gather.12.cloned.1.call-start = ((), (), s32[]{:S(2)}) async-start(), calls=%async_computation.14 | async-start | bytes 4055040 | tf_op jit(solution)/shard_map/all_gather | solution.py:131
  9.4 248.6 %all-gather.14.cloned.1.call-start = ((), (), s32[]{:S(2)}) async-start(), calls=%async_computation.15 | async-start | bytes 3133440 | tf_op jit(solution)/shard_map/all_gather | solution.py:143
  10.0 345.2 %all-gather.20.cloned.1.call-start = ((), (), s32[]{:S(2)}) async-start(), calls=%async_computation.18 | async-start | bytes 6963200 | tf_op jit(solution)/shard_map/all_gather | solution.py:145
  10.6 366.5 %reduce-scatter.15.cloned.1.call-start = ((), (), s32[]{:S(2)}) async-start(), calls=%async_computation.19 | async-start | bytes 7864320 | tf_op jit(solution)/shard_map/reduce_scatter | solution.py:195
  364.4 460.0 %all-gather.22.cloned.1.call-start = ((), (), s32[]{:S(2)}) async-start(), calls=%async_computation.20 | async-start | bytes 3932160 | tf_op jit(solution)/shard_map/all_gather | solution.py:198
  382.2 442.2 %all-gather.24.cloned.1.call-start = ((), (), s32[]{:S(2)}) async-start(), calls=%async_computation.21 | async-start | bytes 17408000 | tf_op jit(solution)/shard_map/all_gather | solution.py:146
  383.0 457.2 %all-gather.28.cloned.1.call-start = ((), (), s32[]{:S(2)}) async-start(), calls=%async_computation.24 | async-start | bytes 3932160 | tf_op jit(solution)/shard_map/all_gather | solution.py:235
  384.3 606.9 %all-gather.26.cloned.1.call-start = ((), (), s32[]{:S(2)}) async-start(), calls=%async_computation.22 | async-start | bytes 17408000 | tf_op jit(solution)/shard_map/all_gather | solution.py:148
  384.9 795.5 %all-gather.30.cloned.1.call-start = ((), (), s32[]{:S(2)}) async-start(), calls=%async_computation.25 | async-start | bytes 17408000 | tf_op jit(solution)/shard_map/all_gather | solution.py:230
  385.7 823.4 %reduce-scatter.19.cloned.1.call-start = ((), (), s32[]{:S(2)}) async-start(), calls=%async_computation.26 | async-start | bytes 7864320 | tf_op jit(solution)/shard_map/reduce_scatter | solution.py:243
  441.4 73.2 %collective-permute-start.3 = (bf16[160,3200]{1,0:T(8,128)(2,1)S(1)}, bf16[160,3200]{1,0:T(8,128)(2,1)}, u32[]{:S(2)}, u32[]{:S(2)}) collective-permute-start(bf16[160,3200]{1,0:T(8,128)(2,1)S(1)} %collective-permute-done.1), channel_id=1, source_target_pairs={{0,30},{2,0},{4,2},{6,4},{8,6},{10,8},{12,10},{14,12},{16,14},{18,... | collective-permute-start | bytes 3072008 | tf_op jit(solution)/shard_map/ppermute | solution.py:31
  568.8 74.8 %collective-permute-start.7 = (bf16[160,3200]{1,0:T(8,128)(2,1)S(1)}, bf16[160,3200]{1,0:T(8,128)(2,1)S(1)}, u32[]{:S(2)}, u32[]{:S(2)}) collective-permute-start(bf16[160,3200]{1,0:T(8,128)(2,1)S(1)} %collective-permute-done.5), channel_id=1, source_target_pairs={{0,30},{2,0},{4,2},{6,4},{8,6},{10,8},{12,10},{14,12},{16,14},{18,... | collective-permute-start | bytes 3072008 | tf_op jit(solution)/shard_map/ppermute | solution.py:31
  620.7 72.0 %collective-permute-start.8 = (bf16[160,3200]{1,0:T(8,128)(2,1)}, bf16[160,3200]{1,0:T(8,128)(2,1)S(1)}, u32[]{:S(2)}, u32[]{:S(2)}) collective-permute-start(bf16[160,3200]{1,0:T(8,128)(2,1)} %collective-permute-done.6), channel_id=1, source_target_pairs={{0,2},{2,4},{4,6},{6,8},{8,10},{10,12},{12,14},{14,16},{16,18},{18... | collective-permute-start | bytes 3072008 | tf_op jit(solution)/shard_map/ppermute | solution.py:26
  1214.5 193.8 %reduce-scatter.25.cloned.1.call-start = ((), (), s32[]{:S(2)}) async-start(), calls=%async_computation.30 | async-start | bytes 98304 | tf_op jit(solution)/shard_map/reduce_scatter | solution.py:282
  1394.2 200.8 %reduce-scatter.17.cloned.1.call-start = ((), (), s32[]{:S(2)}) async-start(), calls=%async_computation.23 | async-start | bytes 3932160 | tf_op jit(solution)/shard_map/reduce_scatter | solution.py:205
  1408.0 192.8 %reduce-scatter.29.cloned.1.call-start = ((), (), s32[]{:S(2)}) async-start(), calls=%async_computation.32 | async-start | bytes 4055040 | tf_op jit(solution)/shard_map/reduce_scatter | solution.py:300
  1414.7 202.8 %reduce-scatter.33.cloned.1.call-start = ((), (), s32[]{:S(2)}) async-start(), calls=%async_computation.34 | async-start | bytes 2785280 | tf_op jit(solution)/shard_map/reduce_scatter | solution.py:308
  1419.9 353.5 %reduce-scatter.31.cloned.1.call-start = ((), (), s32[]{:S(2)}) async-start(), calls=%async_computation.33 | async-start | bytes 6266880 | tf_op jit(solution)/shard_map/reduce_scatter | solution.py:307
  1427.3 475.1 %reduce-scatter.27.cloned.1.call-start = ((), (), s32[]{:S(2)}) async-start(), calls=%async_computation.31 | async-start | bytes 8110080 | tf_op jit(solution)/shard_map/reduce_scatter | solution.py:299
  1435.7 746.4 %reduce-scatter.35.cloned.1.call-start = ((), (), s32[]{:S(2)}) async-start(), calls=%async_computation.35 | async-start | bytes 13926400 | tf_op jit(solution)/shard_map/reduce_scatter | solution.py:309
  1446.2 1412.0 %reduce-scatter.37.cloned.1.call-start = ((), (), s32[]{:S(2)}) async-start(), calls=%async_computation.36 | async-start | bytes 34816000 | tf_op jit(solution)/shard_map/reduce_scatter | solution.py:310
  1464.8 2069.5 %reduce-scatter.39.cloned.1.call-start = ((), (), s32[]{:S(2)}) async-start(), calls=%async_computation.37 | async-start | bytes 34816000 | tf_op jit(solution)/shard_map/reduce_scatter | solution.py:311
  1482.7 2727.9 %reduce-scatter.41.cloned.1.call-start = ((), (), s32[]{:S(2)}) async-start(), calls=%async_computation.38 | async-start | bytes 34816000 | tf_op jit(solution)/shard_map/reduce_scatter | solution.py:312
  (85 other events, 4526.7 us)
Sparse Core Ops, SparseCore 0:
  10.9 56.4 all-gather.15
  70.1 55.4 all-gather.17
  128.5 61.0 all-gather.11
  192.3 65.7 all-gather.13
  260.6 94.5 all-gather.19
  364.5 12.5 reduce-scatter.14
  382.3 12.4 all-gather.21
  397.9 378.7 all-gather.23
  778.3 11.7 all-gather.27
  793.0 198.2 all-gather.25
  994.3 186.1 all-gather.29
  1195.4 13.5 reduce-scatter.18
  1214.6 12.5 all-gather.31
  1394.0 9.1 reduce-scatter.22
  1405.9 10.2 reduce-scatter.20
  1418.3 11.4 reduce-scatter.16
  1436.5 104.6 reduce-scatter.28
  1544.2 73.2 reduce-scatter.32
  1624.0 149.2 reduce-scatter.30
  1780.6 121.7 reduce-scatter.26
  1905.3 276.7 reduce-scatter.34
  2185.0 673.1 reduce-scatter.36
  2861.1 673.1 reduce-scatter.38
  3537.3 673.1 reduce-scatter.40
  (1 shorter events, 8.5 us)
